TPU v7x, 32 devices: a whole 2x2x4 slice. The times are simulated.
32 devices in a mesh: col: 8 (over y, x, core), row: 4 (over z).
Axes of the slice: x: 2, y: 2, z: 4, core: 2. Of those that a mesh axis runs over, the one named last changes fastest.
Arguments:
- matrix: float32 [16, 512, 4096], P(None, 'row', 'col'), may hold values from -0.4 to 2.4, as said below
- pivots: int32 [8, 512], replicated, may hold values from 0 to 511, as said below
- seeds: float32 [8, 512, 512], P('col'), may hold values from -1 to 2, as said below
Outputs:
- factors: float32 [16, 512, 4096], P(None, 'row', 'col')
Inputs may be any that keep to these rules, and one draw needn't show every extreme that they name: Each row of pivots is an ordering of 0 .. 511. Block (r, j) of matrix is zero where r and j differ by more than 8. seeds[k] approximates the inverse of block (k, k) of matrix after the replacement of rows by pivots[k].
All inputs are finite; a program needn't handle non-finite values.
Results may differ from a plain program's by a relative error of at most 0.0001.
Values sent between devices are 32-bit elements; how exact they have to be, the bound alone decides.
A program may use at most 64 MiB of HBM per device.

v0:
```python
import jax
import jax.numpy as jnp
from jax import lax
from jax.sharding import PartitionSpec as P

HB = 8
SWEEPS = 2


def from_root(block, axis, source):
    block = jnp.where(lax.axis_index(axis) == source, block, jnp.zeros_like(block))
    return lax.psum(block, axis)


def dot_high(left, right):
    return jnp.dot(left, right, precision=lax.Precision.HIGHEST, preferred_element_type=jnp.float32)


def refine(pivot_block, approx, identity):
    for sweep_index in range(SWEEPS):
        approx = dot_high(approx, 2.0 * identity - dot_high(pivot_block, approx))
    return approx


def local(matrix, pivots, seeds):
    col_count = lax.axis_size("col")
    col_index = lax.axis_index("col")
    row_index = lax.axis_index("row")
    row_share = matrix.shape[1]
    panel_width = matrix.shape[2]
    identity = jnp.eye(panel_width, dtype=jnp.float32)
    seed_block = seeds[0]

    def eliminate(panel_index, factors):
        local_row = lax.dynamic_index_in_dim(factors, panel_index, 0, keepdims=False)
        block_row = lax.all_gather(local_row, "row", axis=0, tiled=True)
        ordering = lax.dynamic_index_in_dim(pivots, panel_index, 0, keepdims=False)
        swapped = jnp.take(block_row, ordering, axis=0)
        block_row = jnp.where(col_index >= panel_index, swapped, block_row)
        local_row = lax.dynamic_slice_in_dim(block_row, row_index * row_share, row_share, 0)
        factors = lax.dynamic_update_index_in_dim(factors, local_row, panel_index, 0)
        is_owner = col_index == panel_index
        approx = lax.cond(
            is_owner, lambda: refine(block_row, seed_block, identity), lambda: seed_block
        )
        below_rows = lax.dynamic_slice_in_dim(factors, panel_index + 1, HB, 0)
        below_flat = below_rows.reshape(HB * row_share, panel_width)
        scaled = lax.cond(is_owner, lambda: dot_high(below_flat, approx), lambda: below_flat)
        in_reach = (col_index > panel_index) & (col_index <= panel_index + HB)
        arrived = from_root(scaled, "col", panel_index)
        updated = below_flat - dot_high(arrived, block_row)
        result = jnp.where(is_owner, scaled, jnp.where(in_reach, updated, below_flat))
        return lax.dynamic_update_slice_in_dim(
            factors, result.reshape(HB, row_share, panel_width), panel_index + 1, 0
        )

    return lax.fori_loop(0, col_count, eliminate, matrix)


def solution(mesh):
    return jax.shard_map(
        local,
        mesh=mesh,
        in_specs=(P(None, "row", "col"), P(), P("col", None, None)),
        out_specs=P(None, "row", "col"),
        check_vma=False,
    )
```

profile of v0, /device:TPU:31, one launch (start us, length us, event | category | flops | bytes accessed | tf_op | source)
XLA Modules:
  0.0 1025.6 jit_solution(17869282881997952237)
XLA Ops:
  11.4 1007.6 %while.17 = (s32[]{:T(128)}, f32[16,128,512]{2,1,0:T(8,128)}, s32[]{:T(128)}, s32[8,512]{1,0:T(8,128)}, s32[]{:T(128)}, /*index=5*/f32[512,512]{1,0:T(8,128)S(1)...) while((s32[]{:T(128)}, f32[16,128,512]{2,1,0:T(8,128)}, ...), condition=%wide.region_6.7_spmd.clone.clone, body=%wide.region_0.6_spmd.clone.clone.sunk | while | flops 12889626624 | bytes 111953976 | solution.py:57
  15.0 26.2 %all-gather.6.cloned.1.call-done = f32[1,512,512]{2,1,0:T(8,128)} async-done(((f32[1,128,512]{2,1,0:T(8,128)}), f32[1,512,512]{2,1,0:T(8,128)}) %all-gather.6.cloned.1.call-update) | async-done | bytes 1048592 | tf_op jit(solution)/shard_map/while/body/eval_jaxpr/all_gather | solution.py:36
  53.3 75.4 %all-reduce.2.cloned.1.call-done = f32[1024,512]{1,0:T(8,128)} async-done(((f32[1024,512]{1,0:T(8,128)}), f32[1024,512]{1,0:T(8,128)}) %all-reduce.2.cloned.1.call-update) | async-done | bytes 2097168 | tf_op jit(solution)/shard_map/while/body/eval_jaxpr/psum | solution.py:12
  139.9 27.0 %all-gather.6.cloned.1.call-done = f32[1,512,512]{2,1,0:T(8,128)} async-done(((f32[1,128,512]{2,1,0:T(8,128)}), f32[1,512,512]{2,1,0:T(8,128)}) %all-gather.6.cloned.1.call-update) | async-done | bytes 1048592 | tf_op jit(solution)/shard_map/while/body/eval_jaxpr/all_gather | solution.py:36
  178.9 74.8 %all-reduce.2.cloned.1.call-done = f32[1024,512]{1,0:T(8,128)} async-done(((f32[1024,512]{1,0:T(8,128)}), f32[1024,512]{1,0:T(8,128)}) %all-reduce.2.cloned.1.call-update) | async-done | bytes 2097168 | tf_op jit(solution)/shard_map/while/body/eval_jaxpr/psum | solution.py:12
  253.7 5.3 fusion.27
  264.9 26.1 %all-gather.6.cloned.1.call-done = f32[1,512,512]{2,1,0:T(8,128)} async-done(((f32[1,128,512]{2,1,0:T(8,128)}), f32[1,512,512]{2,1,0:T(8,128)}) %all-gather.6.cloned.1.call-update) | async-done | bytes 1048592 | tf_op jit(solution)/shard_map/while/body/eval_jaxpr/all_gather | solution.py:36
  303.0 76.3 %all-reduce.2.cloned.1.call-done = f32[1024,512]{1,0:T(8,128)} async-done(((f32[1024,512]{1,0:T(8,128)}), f32[1024,512]{1,0:T(8,128)}) %all-reduce.2.cloned.1.call-update) | async-done | bytes 2097168 | tf_op jit(solution)/shard_map/while/body/eval_jaxpr/psum | solution.py:12
  390.5 26.8 %all-gather.6.cloned.1.call-done = f32[1,512,512]{2,1,0:T(8,128)} async-done(((f32[1,128,512]{2,1,0:T(8,128)}), f32[1,512,512]{2,1,0:T(8,128)}) %all-gather.6.cloned.1.call-update) | async-done | bytes 1048592 | tf_op jit(solution)/shard_map/while/body/eval_jaxpr/all_gather | solution.py:36
  429.3 75.9 %all-reduce.2.cloned.1.call-done = f32[1024,512]{1,0:T(8,128)} async-done(((f32[1024,512]{1,0:T(8,128)}), f32[1024,512]{1,0:T(8,128)}) %all-reduce.2.cloned.1.call-update) | async-done | bytes 2097168 | tf_op jit(solution)/shard_map/while/body/eval_jaxpr/psum | solution.py:12
  505.3 5.3 fusion.27
  516.5 26.4 %all-gather.6.cloned.1.call-done = f32[1,512,512]{2,1,0:T(8,128)} async-done(((f32[1,128,512]{2,1,0:T(8,128)}), f32[1,512,512]{2,1,0:T(8,128)}) %all-gather.6.cloned.1.call-update) | async-done | bytes 1048592 | tf_op jit(solution)/shard_map/while/body/eval_jaxpr/all_gather | solution.py:36
  554.9 76.4 %all-reduce.2.cloned.1.call-done = f32[1024,512]{1,0:T(8,128)} async-done(((f32[1024,512]{1,0:T(8,128)}), f32[1024,512]{1,0:T(8,128)}) %all-reduce.2.cloned.1.call-update) | async-done | bytes 2097168 | tf_op jit(solution)/shard_map/while/body/eval_jaxpr/psum | solution.py:12
  642.5 26.8 %all-gather.6.cloned.1.call-done = f32[1,512,512]{2,1,0:T(8,128)} async-done(((f32[1,128,512]{2,1,0:T(8,128)}), f32[1,512,512]{2,1,0:T(8,128)}) %all-gather.6.cloned.1.call-update) | async-done | bytes 1048592 | tf_op jit(solution)/shard_map/while/body/eval_jaxpr/all_gather | solution.py:36
  681.3 75.9 %all-reduce.2.cloned.1.call-done = f32[1024,512]{1,0:T(8,128)} async-done(((f32[1024,512]{1,0:T(8,128)}), f32[1024,512]{1,0:T(8,128)}) %all-reduce.2.cloned.1.call-update) | async-done | bytes 2097168 | tf_op jit(solution)/shard_map/while/body/eval_jaxpr/psum | solution.py:12
  757.2 5.3 fusion.27
  768.4 26.4 %all-gather.6.cloned.1.call-done = f32[1,512,512]{2,1,0:T(8,128)} async-done(((f32[1,128,512]{2,1,0:T(8,128)}), f32[1,512,512]{2,1,0:T(8,128)}) %all-gather.6.cloned.1.call-update) | async-done | bytes 1048592 | tf_op jit(solution)/shard_map/while/body/eval_jaxpr/all_gather | solution.py:36
  806.8 77.2 %all-reduce.2.cloned.1.call-done = f32[1024,512]{1,0:T(8,128)} async-done(((f32[1024,512]{1,0:T(8,128)}), f32[1024,512]{1,0:T(8,128)}) %all-reduce.2.cloned.1.call-update) | async-done | bytes 2097168 | tf_op jit(solution)/shard_map/while/body/eval_jaxpr/psum | solution.py:12
  895.3 26.7 %all-gather.6.cloned.1.call-done = f32[1,512,512]{2,1,0:T(8,128)} async-done(((f32[1,128,512]{2,1,0:T(8,128)}), f32[1,512,512]{2,1,0:T(8,128)}) %all-gather.6.cloned.1.call-update) | async-done | bytes 1048592 | tf_op jit(solution)/shard_map/while/body/eval_jaxpr/all_gather | solution.py:36
  928.2 11.3 %conditional.8 = (f32[512,512]{1,0:T(8,128)}) conditional(s32[]{:T(128)} %convert_element_type.27, f32[512,512]{1,0:T(8,128)S(1)} %get-tuple-element.345, (f32[512,512]{1,0:T(8,128)}, f32[512,512]{1,0:T(8,128)}, f32[512,512]{1,0:T(8,128)S(1)}, f32[512,512]{1,0:T(8,128)S(1)}) %tuple.77), branch_computations={%region_1.1_spmd, %region_2.2_spmd} | conditional | flops 6443499520 | bytes 18874404 | solution.py:43
  941.4 6.0 conditional.9
  941.4 6.0 fusion.5
  950.6 60.3 %all-reduce.2.cloned.1.call-done = f32[1024,512]{1,0:T(8,128)} async-done(((f32[1024,512]{1,0:T(8,128)}), f32[1024,512]{1,0:T(8,128)}) %all-reduce.2.cloned.1.call-update) | async-done | bytes 2097168 | tf_op jit(solution)/shard_map/while/body/eval_jaxpr/psum | solution.py:12
  1010.8 5.9 fusion.27
  (225 shorter events, 195.4 us)
Async XLA Ops:
  11.4 29.8 %all-gather.6.cloned.1.call-start = ((), (), s32[]{:S(2)}) async-start(), calls=%async_computation | async-start | bytes 1310720 | tf_op jit(solution)/shard_map/while/body/eval_jaxpr/all_gather | solution.py:36
  13.1 115.6 %all-reduce.2.cloned.1.call-start = ((), (), s32[]{:S(2)}) async-start(), calls=%async_computation.1 | async-start | bytes 4194304 | tf_op jit(solution)/shard_map/while/body/eval_jaxpr/psum | solution.py:12
  128.7 5.3 copy-start.4
  136.3 30.6 %all-gather.6.cloned.1.call-start = ((), (), s32[]{:S(2)}) async-start(), calls=%async_computation | async-start | bytes 1310720 | tf_op jit(solution)/shard_map/while/body/eval_jaxpr/all_gather | solution.py:36
  138.0 115.7 %all-reduce.2.cloned.1.call-start = ((), (), s32[]{:S(2)}) async-start(), calls=%async_computation.1 | async-start | bytes 4194304 | tf_op jit(solution)/shard_map/while/body/eval_jaxpr/psum | solution.py:12
  253.7 5.3 copy-start.4
  261.2 29.7 %all-gather.6.cloned.1.call-start = ((), (), s32[]{:S(2)}) async-start(), calls=%async_computation | async-start | bytes 1310720 | tf_op jit(solution)/shard_map/while/body/eval_jaxpr/all_gather | solution.py:36
  262.9 116.4 %all-reduce.2.cloned.1.call-start = ((), (), s32[]{:S(2)}) async-start(), calls=%async_computation.1 | async-start | bytes 4194304 | tf_op jit(solution)/shard_map/while/body/eval_jaxpr/psum | solution.py:12
  379.3 5.3 copy-start.4
  386.9 30.4 %all-gather.6.cloned.1.call-start = ((), (), s32[]{:S(2)}) async-start(), calls=%async_computation | async-start | bytes 1310720 | tf_op jit(solution)/shard_map/while/body/eval_jaxpr/all_gather | solution.py:36
  388.6 116.7 %all-reduce.2.cloned.1.call-start = ((), (), s32[]{:S(2)}) async-start(), calls=%async_computation.1 | async-start | bytes 4194304 | tf_op jit(solution)/shard_map/while/body/eval_jaxpr/psum | solution.py:12
  505.3 5.3 copy-start.4
  512.9 30.0 %all-gather.6.cloned.1.call-start = ((), (), s32[]{:S(2)}) async-start(), calls=%async_computation | async-start | bytes 1310720 | tf_op jit(solution)/shard_map/while/body/eval_jaxpr/all_gather | solution.py:36
  514.6 116.7 %all-reduce.2.cloned.1.call-start = ((), (), s32[]{:S(2)}) async-start(), calls=%async_computation.1 | async-start | bytes 4194304 | tf_op jit(solution)/shard_map/while/body/eval_jaxpr/psum | solution.py:12
  631.3 5.3 copy-start.4
  638.8 30.5 %all-gather.6.cloned.1.call-start = ((), (), s32[]{:S(2)}) async-start(), calls=%async_computation | async-start | bytes 1310720 | tf_op jit(solution)/shard_map/while/body/eval_jaxpr/all_gather | solution.py:36
  640.5 116.7 %all-reduce.2.cloned.1.call-start = ((), (), s32[]{:S(2)}) async-start(), calls=%async_computation.1 | async-start | bytes 4194304 | tf_op jit(solution)/shard_map/while/body/eval_jaxpr/psum | solution.py:12
  757.2 5.3 copy-start.4
  764.8 30.0 %all-gather.6.cloned.1.call-start = ((), (), s32[]{:S(2)}) async-start(), calls=%async_computation | async-start | bytes 1310720 | tf_op jit(solution)/shard_map/while/body/eval_jaxpr/all_gather | solution.py:36
  766.5 117.6 %all-reduce.2.cloned.1.call-start = ((), (), s32[]{:S(2)}) async-start(), calls=%async_computation.1 | async-start | bytes 4194304 | tf_op jit(solution)/shard_map/while/body/eval_jaxpr/psum | solution.py:12
  884.1 5.3 copy-start.4
  891.6 30.4 %all-gather.6.cloned.1.call-start = ((), (), s32[]{:S(2)}) async-start(), calls=%async_computation | async-start | bytes 1310720 | tf_op jit(solution)/shard_map/while/body/eval_jaxpr/all_gather | solution.py:36
  893.3 117.5 %all-reduce.2.cloned.1.call-start = ((), (), s32[]{:S(2)}) async-start(), calls=%async_computation.1 | async-start | bytes 4194304 | tf_op jit(solution)/shard_map/while/body/eval_jaxpr/psum | solution.py:12
  1010.8 5.9 copy-start.4
  (26 other events, 75.5 us)
Sparse Core Ops, SparseCore 0:
  13.8 27.4 all-gather.5
  53.4 75.2 all-reduce.1
  138.7 28.1 all-gather.5
  179.0 74.6 all-reduce.1
  263.3 27.6 all-gather.5
  303.1 76.1 all-reduce.1
  389.3 28.0 all-gather.5
  429.5 75.7 all-reduce.1
  515.2 27.6 all-gather.5
  555.0 76.2 all-reduce.1
  641.2 28.0 all-gather.5
  681.4 75.7 all-reduce.1
  767.2 27.6 all-gather.5
  806.9 77.0 all-reduce.1
  893.7 28.2 all-gather.5
  950.7 60.1 all-reduce.1
where the time goes:
time: 1030 us
  waiting for transfers between devices  805 us (78%)
  local copies, waits for them, and re-layouts  106 us (10%)
  matrix products  60 us (6%)
  other arithmetic  39.8 us (4%)
  between operations  13.1 us (1%)
    psum x8, waiting for transfers between devices, from_root(): return lax.psum(block, axis)  592 us
    all_gather x8, waiting for transfers between devices, eliminate(): block_row = lax.all_gather(local_row, 'row', axis=0, tiled=True)  213 us
    dot_general x13, matrix products, dot_high(): jnp.dot(left, right, precision=lax.Precision.HIGHEST, preferred_element_t...  60 us
    gather x8, local copies, waits for them, and re-layouts, eliminate(): swapped = jnp.take(block_row, ordering, axis=0)  32.5 us
  transfers between devices with their start and end apart: 16, of which 16 were waited for; matrix products, arithmetic and copies ran while one was open for 1% of the time, Pallas kernels for 0%

commit v1 on v0

v1 whole, which is shorter than its diff:
```python
import functools

import jax
import jax.numpy as jnp
from jax import lax
from jax.experimental import pallas as pl
from jax.experimental.pallas import tpu as pltpu
from jax.sharding import PartitionSpec as P

HB = 8
SWEEPS = 2
F32 = jnp.float32
BF16 = jnp.bfloat16
MESH = pl.DeviceIdType.MESH


def split(x):
    high = x.astype(BF16)
    return high, (x - high.astype(F32)).astype(BF16)


def dot(left, right):
    return jnp.dot(left, right, preferred_element_type=F32)


def dot3(left, right):
    return dot(left[0], right[0]) + (dot(left[0], right[1]) + dot(left[1], right[0]))


def split3(x):
    high, rest = split(x)
    middle = rest
    return high, middle, (x - high.astype(F32) - middle.astype(F32)).astype(BF16)


def kernel(
    ncol, nrow, a_hbm, pivc_ref, pivr_ref, seed_ref, out_ref,
    upper, mult, u_high, u_low, approx, y_high, y_low,
    usend, urecv, msend, mrecv, lsem,
):
    col = lax.axis_index("col")
    row = lax.axis_index("row")
    right = lax.rem(col + 1, ncol)
    left = lax.rem(col + ncol - 1, ncol)
    share, width = out_ref.shape[1], out_ref.shape[2]
    first = jnp.maximum(col - HB, 0)

    load = pltpu.make_async_copy(a_hbm, out_ref, lsem)
    load.start()
    barrier = pltpu.get_barrier_semaphore()
    for step in range(1, nrow):
        pl.semaphore_signal(
            barrier, inc=1, device_id=(col, lax.rem(row + step, nrow)), device_id_type=MESH
        )
    for side in (left, right):
        pl.semaphore_signal(barrier, inc=1, device_id=(side, row), device_id_type=MESH)
    pl.semaphore_wait(barrier, nrow + 1)
    load.wait()

    def share_copy(k, step, source, target):
        return pltpu.make_async_remote_copy(
            src_ref=upper.at[k, source],
            dst_ref=upper.at[k, source],
            send_sem=usend.at[k, step],
            recv_sem=urecv.at[k, source],
            device_id=(col, target),
            device_id_type=MESH,
        )

    def start_gather(k):
        upper[k, row] = out_ref[k]
        for step in range(1, nrow):
            share_copy(k, step, row, lax.rem(row + step, nrow)).start()

    def finish_gather(k):
        for step in range(1, nrow):
            source = lax.rem(row + step, nrow)
            share_copy(k, step, source, source).wait_recv()

    def mult_copy(k, c):
        return pltpu.make_async_remote_copy(
            src_ref=mult.at[k, c],
            dst_ref=mult.at[k, c],
            send_sem=msend.at[k, c],
            recv_sem=mrecv.at[k, c],
            device_id=(right, row),
            device_id_type=MESH,
        )

    def store_swapped(k):
        picks = lax.broadcasted_iota(jnp.int32, (share, width), 1) == pivc_ref[k]
        picks = jnp.where(picks, 1.0, 0.0).astype(BF16)
        parts = split3(upper[k].reshape(width, width))
        out_ref[k] = dot(picks, parts[0]) + (dot(picks, parts[1]) + dot(picks, parts[2]))

    def split_upper(k):
        high, low = split(upper[k].reshape(width, width))
        u_high[...] = high
        u_low[...] = low

    start_gather(first)

    ordering = jnp.broadcast_to(pivr_ref[col], (width, width))
    scatter = lax.broadcasted_iota(jnp.int32, (width, width), 0) == ordering
    scatter = jnp.where(scatter, 1.0, 0.0).astype(BF16)
    seed_parts = split3(seed_ref[0])
    contract = (((1,), (1,)), ((), ()))
    total = lax.dot_general(seed_parts[2], scatter, contract, preferred_element_type=F32)
    total += lax.dot_general(seed_parts[1], scatter, contract, preferred_element_type=F32)
    total += lax.dot_general(seed_parts[0], scatter, contract, preferred_element_type=F32)
    approx[...] = total

    def update(k, carry):
        finish_gather(k)
        split_upper(k)
        store_swapped(k)
        passes_on = (col + 1 < ncol) & (col + 1 <= k + HB)

        def chunk(c):
            copy = mult_copy(k, c)
            copy.wait_recv()

            @pl.when(passes_on)
            def _():
                copy.start()

            change = dot3(split(mult[k, c]), (u_high[...], u_low[...]))
            out_ref[k + 1 + c] = out_ref[k + 1 + c] - change

        chunk(0)
        start_gather(k + 1)

        @pl.loop(1, HB)
        def _(c):
            chunk(c)

        return carry

    lax.fori_loop(first, col, update, 0)

    finish_gather(col)
    split_upper(col)
    diagonal = lax.broadcasted_iota(jnp.int32, (width, width), 0)
    diagonal = diagonal == lax.broadcasted_iota(jnp.int32, (width, width), 1)

    @pl.loop(0, SWEEPS)
    def _(sweep):
        parts = split(approx[...])
        product = dot3((u_high[...], u_low[...]), parts)
        approx[...] = dot3(parts, split(jnp.where(diagonal, 2.0, 0.0) - product))

    high, low = split(approx[...])
    y_high[...] = high
    y_low[...] = low

    @pl.loop(0, HB)
    def _(c):
        mult[col, c] = dot3(split(out_ref[col + 1 + c]), (y_high[...], y_low[...]))

        @pl.when(col + 1 < ncol)
        def _():
            mult_copy(col, c).start()

    store_swapped(col)
    y_high[...] = scatter

    @pl.loop(0, HB)
    def _(c):
        parts = split3(mult[col, c])
        target = y_high[...]
        out_ref[col + 1 + c] = dot(parts[0], target) + (dot(parts[1], target) + dot(parts[2], target))

    def drain(k, carry):
        for step in range(1, nrow):
            share_copy(k, step, row, lax.rem(row + step, nrow)).wait_send()

        @pl.when((col + 1 < ncol) & (col + 1 <= k + HB))
        def _():
            @pl.loop(0, HB)
            def _(c):
                mult_copy(k, c).wait_send()

        return carry

    lax.fori_loop(first, col + 1, drain, 0)


def local(matrix, pivots, seeds):
    ncol = lax.axis_size("col")
    nrow = lax.axis_size("row")
    nblk, share, width = matrix.shape
    start = lax.axis_index("row") * share
    by_row = lax.dynamic_slice_in_dim(pivots, start, share, 1)[:, :, None]
    by_col = pivots[:, None, :]
    vmem = pl.BlockSpec(memory_space=pltpu.VMEM)
    return pl.pallas_call(
        functools.partial(kernel, ncol, nrow),
        out_shape=jax.ShapeDtypeStruct(matrix.shape, F32),
        in_specs=[pl.BlockSpec(memory_space=pl.ANY), vmem, vmem, vmem],
        out_specs=vmem,
        scratch_shapes=[
            pltpu.VMEM((ncol, nrow, share, width), F32),
            pltpu.VMEM((ncol, HB, share, width), F32),
            pltpu.VMEM((width, width), BF16),
            pltpu.VMEM((width, width), BF16),
            pltpu.VMEM((width, width), F32),
            pltpu.VMEM((width, width), BF16),
            pltpu.VMEM((width, width), BF16),
            pltpu.SemaphoreType.DMA((ncol, nrow)),
            pltpu.SemaphoreType.DMA((ncol, nrow)),
            pltpu.SemaphoreType.DMA((ncol, HB)),
            pltpu.SemaphoreType.DMA((ncol, HB)),
            pltpu.SemaphoreType.DMA,
        ],
        compiler_params=pltpu.CompilerParams(
            collective_id=0, has_side_effects=True, vmem_limit_bytes=60 * 1024 * 1024
        ),
    )(matrix, by_row, by_col, seeds)


def solution(mesh):
    return jax.shard_map(
        local,
        mesh=mesh,
        in_specs=(P(None, "row", "col"), P(), P("col", None, None)),
        out_specs=P(None, "row", "col"),
        check_vma=False,
    )
```

time: 1030 us -> 239 us (0.23)
  waiting for transfers between devices: 805 us -> 0 us
  Pallas kernels: 0 us -> 231 us
  local copies, waits for them, and re-layouts: 106 us -> 7.84 us
  matrix products: 60 us -> 0 us
  other arithmetic: 39.8 us -> 0 us
  between operations: 13.1 us -> 0.01 us
    psum x8 -> x0, waiting for transfers between devices: 592 us -> none  [from_root(): return lax.psum(block, axis)]
    pallas_call x0 -> x1, Pallas kernels: none -> 231 us  [local(): pl.pallas_call(functools.partial(kernel, ncol, nrow), out_shape=jax.Shape...]
    all_gather x8 -> x0, waiting for transfers between devices: 213 us -> none  [eliminate(): block_row = lax.all_gather(local_row, 'row', axis=0, tiled=True)]
    dot_general x13 -> x0, matrix products: 60 us -> none  [dot_high(): jnp.dot(left, right, precision=lax.Precision.HIGHEST, preferred_element_t...]
    gather x8 -> x0, local copies, waits for them, and re-layouts: 32.5 us -> none  [eliminate(): swapped = jnp.take(block_row, ordering, axis=0)]
    select_n x24 -> x0, other arithmetic: 30.9 us -> none  [the longest x8 13.9 us: from_root(): jnp.where(lax.axis_index(axis) == source, block, jnp.zeros_like(block))]
    dynamic_slice x16 -> x0, local copies, waits for them, and re-layouts: 28.3 us -> none  [the longest x8 14.9 us: eliminate(): below_rows = lax.dynamic_slice_in_dim(factors, panel_index + 1, HB, 0)]
    cond x16 -> x0, local copies, waits for them, and re-layouts: 16.4 us -> none
  transfers between devices with their start and end apart: 16 -> 0, of which waited for: 16 -> 0; matrix products, arithmetic and copies ran while one was open for 1% -> 0% of each run, Pallas kernels for 0% -> 0%
where the time goes in v1:
time: 239 us
  Pallas kernels  231 us (97%)
  local copies, waits for them, and re-layouts  7.84 us (3%)
    pallas_call x1, Pallas kernels, local(): pl.pallas_call(functools.partial(kernel, ncol, nrow), out_shape=jax.Shape...  231 us
    unnamed x1, local copies, waits for them, and re-layouts  4.81 us

profile of v1, /device:TPU:31, one launch (start us, length us, event | category | flops | bytes accessed | tf_op | source)
XLA Modules:
  0.0 238.8 jit_solution(8207902355590177423)
XLA Ops:
  0.0 0.7 dynamic-slice_bitcast_fusion
  0.7 1.3 broadcast_in_dim.7.pivr_ref
  2.0 1.0 copy.4.pivc_ref
  3.0 230.9 %shard_map.37 = f32[16,128,512]{2,1,0:T(8,128)} custom-call(f32[16,128,512]{2,1,0:T(8,128)} %a_hbm.1, s32[8,128,1]{2,1,0:T(8,128)} %copy.4.pivc_ref, s32[8,1,512]{2,1,0:T(1,128)} %broadcast_in_dim.7.pivr_ref, f32[1,512,512]{2,1,0:T(8,128)} %seed_ref.1), custom_call_target="tpu_custom_call" | custom-call | tf_op jit(solution)/shard_map/pallas_call | solution.py:196
  234.0 4.8 %copy.6 = f32[16,128,512]{2,1,0:T(8,128)} copy(f32[16,128,512]{2,1,0:T(8,128)} %shard_map.37) | data formatting | bytes 8388608

commit v2 on v1

--- a/solution.py
+++ b/solution.py
@@ -9,6 +9,7 @@
 
 HB = 8
 SWEEPS = 2
+CHIPS = 4
 F32 = jnp.float32
 BF16 = jnp.bfloat16
 MESH = pl.DeviceIdType.MESH
@@ -40,8 +41,6 @@
 ):
     col = lax.axis_index("col")
     row = lax.axis_index("row")
-    right = lax.rem(col + 1, ncol)
-    left = lax.rem(col + ncol - 1, ncol)
     share, width = out_ref.shape[1], out_ref.shape[2]
     first = jnp.maximum(col - HB, 0)
 
@@ -52,9 +51,11 @@
         pl.semaphore_signal(
             barrier, inc=1, device_id=(col, lax.rem(row + step, nrow)), device_id_type=MESH
         )
-    for side in (left, right):
-        pl.semaphore_signal(barrier, inc=1, device_id=(side, row), device_id_type=MESH)
-    pl.semaphore_wait(barrier, nrow + 1)
+    for step in range(1, ncol):
+        pl.semaphore_signal(
+            barrier, inc=1, device_id=(lax.rem(col + step, ncol), row), device_id_type=MESH
+        )
+    pl.semaphore_wait(barrier, nrow + ncol - 2)
     load.wait()
 
     def share_copy(k, step, source, target):
@@ -77,15 +78,50 @@
             source = lax.rem(row + step, nrow)
             share_copy(k, step, source, source).wait_recv()
 
-    def mult_copy(k, c):
+    paired = ncol == 2 * CHIPS and ncol <= HB + 1
+
+    def mult_copy(k, c, way, target):
         return pltpu.make_async_remote_copy(
             src_ref=mult.at[k, c],
             dst_ref=mult.at[k, c],
-            send_sem=msend.at[k, c],
+            send_sem=msend.at[k, c, way],
             recv_sem=mrecv.at[k, c],
-            device_id=(right, row),
+            device_id=(target, row),
             device_id_type=MESH,
         )
+
+    def routes(k, path):
+        if not paired:
+            return [((col + 1 < ncol) & (col + 1 <= k + HB), lax.rem(col + 1, ncol))]
+        chip, core, owner = col // 2, col % 2, k // 2
+        at_owner = col == k
+        carries = at_owner | ((chip > owner) & (core == path))
+        beside = (at_owner & (core == 0)) | ((chip > owner) & (core == path))
+        if path == 0:
+            onward = [(chip == 0, 1), (chip == 1, 3), ((chip == 3) & (owner < 2), 2),
+                      ((chip == 2) & (owner == 2), 3)]
+        else:
+            onward = [(chip == 0, 2), ((chip == 1) & (owner == 1), 2), (chip == 2, 3),
+                      ((chip == 3) & (owner == 0), 1)]
+        found = onward[0][0]
+        target = 0
+        for test, goal in onward:
+            found = found | test
+            target = target + jnp.where(test, goal, 0)
+        away = lax.rem(2 * target + path, ncol)
+        return [(carries & found, away), (beside, chip * 2 + 1 - core)]
+
+    def pass_on(k, c, path):
+        for way, (test, target) in enumerate(routes(k, path)):
+            @pl.when(test)
+            def _():
+                mult_copy(k, c, way, target).start()
+
+    def drain_sends(k, c, path):
+        for way, (test, target) in enumerate(routes(k, path)):
+            @pl.when(test)
+            def _():
+                mult_copy(k, c, way, target).wait_send()
 
     def store_swapped(k):
         picks = lax.broadcasted_iota(jnp.int32, (share, width), 1) == pivc_ref[k]
@@ -114,25 +150,30 @@
         finish_gather(k)
         split_upper(k)
         store_swapped(k)
-        passes_on = (col + 1 < ncol) & (col + 1 <= k + HB)
-
-        def chunk(c):
-            copy = mult_copy(k, c)
-            copy.wait_recv()
-
-            @pl.when(passes_on)
-            def _():
-                copy.start()
-
+
+        def chunk(c, path):
+            mult_copy(k, c, 0, lax.rem(col + 1, ncol)).wait_recv()
+            pass_on(k, c, path)
             change = dot3(split(mult[k, c]), (u_high[...], u_low[...]))
             out_ref[k + 1 + c] = out_ref[k + 1 + c] - change
 
-        chunk(0)
-        start_gather(k + 1)
-
-        @pl.loop(1, HB)
+        later = (col == k + 2) & (col % 2 == 1) & paired
+        chunk(0, 0)
+
+        @pl.when(jnp.logical_not(later))
+        def _():
+            start_gather(k + 1)
+
+        chunk(1, 1)
+
+        @pl.loop(1, HB // 2)
         def _(c):
-            chunk(c)
+            chunk(2 * c, 0)
+            chunk(2 * c + 1, 1)
+
+        @pl.when(later)
+        def _():
+            start_gather(k + 1)
 
         return carry
 
@@ -153,13 +194,12 @@
     y_high[...] = high
     y_low[...] = low
 
-    @pl.loop(0, HB)
-    def _(c):
-        mult[col, c] = dot3(split(out_ref[col + 1 + c]), (y_high[...], y_low[...]))
-
-        @pl.when(col + 1 < ncol)
-        def _():
-            mult_copy(col, c).start()
+    @pl.loop(0, HB // 2)
+    def _(pair):
+        for path in range(2):
+            c = 2 * pair + path
+            mult[col, c] = dot3(split(out_ref[col + 1 + c]), (y_high[...], y_low[...]))
+            pass_on(col, c, path)
 
     store_swapped(col)
     y_high[...] = scatter
@@ -174,11 +214,10 @@
         for step in range(1, nrow):
             share_copy(k, step, row, lax.rem(row + step, nrow)).wait_send()
 
-        @pl.when((col + 1 < ncol) & (col + 1 <= k + HB))
-        def _():
-            @pl.loop(0, HB)
-            def _(c):
-                mult_copy(k, c).wait_send()
+        @pl.loop(0, HB // 2)
+        def _(pair):
+            for path in range(2):
+                drain_sends(k, 2 * pair + path, path)
 
         return carry
 
@@ -208,7 +247,7 @@
             pltpu.VMEM((width, width), BF16),
             pltpu.SemaphoreType.DMA((ncol, nrow)),
             pltpu.SemaphoreType.DMA((ncol, nrow)),
-            pltpu.SemaphoreType.DMA((ncol, HB)),
+            pltpu.SemaphoreType.DMA((ncol, HB, 2)),
             pltpu.SemaphoreType.DMA((ncol, HB)),
             pltpu.SemaphoreType.DMA,
         ],

time: 239 us -> 438 us (1.83)
  Pallas kernels: 231 us -> 430 us
    pallas_call x1, Pallas kernels: 231 us -> 430 us  [local(): pl.pallas_call(functools.partial(kernel, ncol, nrow), out_shape=jax.Shape...]
where the time goes in v2:
time: 438 us
  Pallas kernels  430 us (98%)
  local copies, waits for them, and re-layouts  7.84 us (2%)
    pallas_call x1, Pallas kernels, local(): pl.pallas_call(functools.partial(kernel, ncol, nrow), out_shape=jax.Shape...  430 us

profile of v2, /device:TPU:31, one launch (start us, length us, event | category | flops | bytes accessed | tf_op | source)
XLA Modules:
  0.0 437.9 jit_solution(877775684273117590)
XLA Ops:
  0.0 0.7 dynamic-slice_bitcast_fusion
  0.7 1.3 broadcast_in_dim.7.pivr_ref
  2.0 1.0 copy.4.pivc_ref
  3.0 430.0 %shard_map.37 = f32[16,128,512]{2,1,0:T(8,128)} custom-call(f32[16,128,512]{2,1,0:T(8,128)} %a_hbm.1, s32[8,128,1]{2,1,0:T(8,128)} %copy.4.pivc_ref, s32[8,1,512]{2,1,0:T(1,128)} %broadcast_in_dim.7.pivr_ref, f32[1,512,512]{2,1,0:T(8,128)} %seed_ref.1), custom_call_target="tpu_custom_call" | custom-call | tf_op jit(solution)/shard_map/pallas_call | solution.py:235
  433.1 4.8 %copy.6 = f32[16,128,512]{2,1,0:T(8,128)} copy(f32[16,128,512]{2,1,0:T(8,128)} %shard_map.37) | data formatting | bytes 8388608
